TPU v7x, 32 devices: a whole 2x2x4 slice. The times are simulated.
32 devices in a mesh: groups: 2 (over y), space: 4 (over z), batch: 4 (over x, core).
Axes of the slice: x: 2, y: 2, z: 4, core: 2. Of those that a mesh axis runs over, the one named last changes fastest.
Arguments:
- fields: bfloat16 [8, 32, 64, 128], P(('groups', 'batch'), 'space'), parts along dimension 0, may hold values from -36 to 36
- land: int32 [32, 64], P('space'), may hold values 0 or 1
- conv_in: bfloat16 [9, 128, 128], replicated, may hold values from -0.1875 to 0.1875
- conv_out: bfloat16 [9, 128, 128], replicated, may hold values from -0.1875 to 0.1875
- batchnorm_gain: float32 [128], replicated, may hold values from 0.25 to 1.75
- batchnorm_offset: float32 [128], replicated, may hold values from -3 to 3
- target_grad: bfloat16 [8, 32, 64, 128], P(('groups', 'batch'), 'space'), parts along dimension 0, may hold values from -6 to 6
Outputs:
- output: bfloat16 [8, 32, 64, 128], P(('groups', 'batch'), 'space'), parts along dimension 0
- grad_in: float32 [18, 128, 128], P('groups', None, 'batch'), parts along dimension 0
- grad_out: float32 [18, 128, 128], P('groups', None, 'batch'), parts along dimension 0
- gain_gradient: float32 [256], P('groups'), parts along dimension 0
- offset_gradient: float32 [256], P('groups'), parts along dimension 0
There are 2 independent parts, one for each index of `groups`. A program takes and returns all parts, laid end to end along the dimension named above; an argument that names none is the same for every part. Nothing has to cross between parts.
All inputs are finite; a program needn't handle non-finite values. No bound on the sum of `land` on one device may be relied on, other than what follows from the above.
Results may differ from a plain program's by a relative error of at most 0.025.
Values may be sent and summed in bfloat16 or wider, within the bound.
No kernel may reach another device: no remote copies, remote signals or barrier semaphores. Data moves between devices by JAX's collectives and lax.ppermute only.
A program may use at most 64 MiB of HBM per device.

v0:
```python
import jax
import jax.numpy as jnp
from jax import lax
from jax.sharding import PartitionSpec as P


def partner(value, axis, distance):
    mask = 2**distance
    pairs = [(source, source ^ mask) for source in range(lax.axis_size(axis))]
    return lax.ppermute(value, axis, pairs)


def extended_2(x, sides, width):
    for axis, dim in sides:
        size, length = (lax.axis_size(axis), x.shape[dim])
        up = [(i, (i + 1) % size) for i in range(size)]
        down = [(j, i) for i, j in up]
        last = lax.slice_in_dim(x, length - width, length, axis=dim)
        initial = lax.slice_in_dim(x, 0, width, axis=dim)
        before = lax.ppermute(last, axis, up)
        after = lax.ppermute(initial, axis, down)
        x = jnp.concatenate([before, x, after], axis=dim)
    return x


def mirror_row(row_part):
    steps_total = lax.axis_size("space").bit_length() - 1
    moved = row_part
    for bit_number in range(steps_total):
        moved = partner(moved, "space", bit_number)
    return jnp.flip(moved, axis=1)


def surround(field):
    ghost = mirror_row(field[:, :, -1, :])
    south = jnp.zeros_like(field[:, :, :1, :])
    extended = jnp.concatenate([south, field, ghost[:, :, None, :]], axis=2)
    return extended_2(extended, (("space", 1),), 1)


def convolve(padded, weights, lon, lat):
    chans = padded.shape[3]
    total = jnp.zeros((padded.shape[0] * lon * lat, weights.shape[2]), jnp.float32)
    for tap in range(9):
        first, second = (tap // 3, tap % 3)
        piece = padded[:, first : first + lon, second : second + lat, :].reshape(-1, chans)
        total = total + jnp.dot(piece, weights[tap], preferred_element_type=jnp.float32)
    return total.reshape(padded.shape[0], lon, lat, weights.shape[2])


def adjoint_conv(padded, weights, lon, lat):
    chans = padded.shape[3]
    ghost_row = padded[:, :, lat + 1, :]
    cleared = padded.at[:, :, lat + 1, :].set(jnp.zeros_like(ghost_row))
    total = jnp.zeros((padded.shape[0] * lon * lat, weights.shape[1]), jnp.float32)
    for tap in range(9):
        first, second = (tap // 3, tap % 3)
        piece = cleared[:, 2 - first : 2 - first + lon, 2 - second : 2 - second + lat, :].reshape(
            -1, chans
        )
        total = total + lax.dot_general(
            piece, weights[tap], (((1,), (1,)), ((), ())), preferred_element_type=jnp.float32
        )
    total = total.reshape(padded.shape[0], lon, lat, weights.shape[1])
    extra = jnp.zeros((padded.shape[0] * lon, weights.shape[1]), jnp.float32)
    for first in range(3):
        piece = ghost_row[:, first : first + lon, :].reshape(-1, chans)
        extra = extra + lax.dot_general(
            piece,
            weights[3 * first + 2],
            (((1,), (1,)), ((), ())),
            preferred_element_type=jnp.float32,
        )
    extra = extra.reshape(padded.shape[0], lon, weights.shape[1])
    return total.at[:, :, lat - 1, :].add(extra)


def tap_grads(padded, grad, lon, lat):
    chans = padded.shape[3]
    flat = grad.reshape(-1, grad.shape[3])
    result = []
    for tap in range(9):
        first, second = (tap // 3, tap % 3)
        piece = padded[:, first : first + lon, second : second + lat, :].reshape(-1, chans)
        result.append(
            lax.dot_general(
                piece, flat, (((0,), (0,)), ((), ())), preferred_element_type=jnp.float32
            )
        )
    return jnp.stack(result, axis=0)


def reduce_weights(partial_grad):
    summed = lax.psum(partial_grad.astype(jnp.bfloat16), "space")
    return lax.psum_scatter(summed, "batch", scatter_dimension=2, tiled=True).astype(jnp.float32)


def gelu_value(value):
    inner = 0.7978845608 * (value + 0.044715 * value * value * value)
    return 0.5 * value * (1.0 + jnp.tanh(inner))


def gelu_slope(value):
    inner = 0.7978845608 * (value + 0.044715 * value * value * value)
    hyper = jnp.tanh(inner)
    return 0.5 * (1.0 + hyper) + 0.5 * value * (1.0 - hyper * hyper) * 0.7978845608 * (
        1.0 + 3.0 * 0.044715 * value * value
    )


def body(fields, land, conv_in, conv_out, batchnorm_gain, batchnorm_offset, target_grad):
    lon, lat = (fields.shape[1], fields.shape[2])
    ocean_mask = land.astype(jnp.float32)[None, :, :, None]
    masked = fields * ocean_mask.astype(jnp.bfloat16)
    padded_in = surround(masked)
    first = convolve(padded_in, conv_in, lon, lat).astype(jnp.bfloat16)
    first_features = first.astype(jnp.float32)
    local_count = jnp.sum(land.astype(jnp.float32)) * fields.shape[0]
    sums, squares, element_count = lax.psum(
        (
            jnp.sum(first_features * ocean_mask, axis=(0, 1, 2)),
            jnp.sum(first_features * first_features * ocean_mask, axis=(0, 1, 2)),
            local_count,
        ),
        ("space", "batch"),
    )
    channel_mean = sums / element_count
    var = squares / element_count - channel_mean * channel_mean
    inverse_deviation = lax.rsqrt(var + 1e-05)
    normalized_input = (first_features - channel_mean) * inverse_deviation
    preactivation = batchnorm_gain * normalized_input + batchnorm_offset
    act = (gelu_value(preactivation) * ocean_mask).astype(jnp.bfloat16)
    padded_act = surround(act)
    output = (convolve(padded_act, conv_out, lon, lat) * ocean_mask).astype(jnp.bfloat16)
    dout = (target_grad.astype(jnp.float32) * ocean_mask * lax.rsqrt(element_count)).astype(
        jnp.bfloat16
    )
    grad_out = reduce_weights(tap_grads(padded_act, dout, lon, lat))
    dact = adjoint_conv(surround(dout), conv_out, lon, lat)
    preactivation_gradient = dact * ocean_mask * gelu_slope(preactivation)
    offset_gradient, gain_gradient = lax.psum(
        (
            jnp.sum(preactivation_gradient, axis=(0, 1, 2)),
            jnp.sum(preactivation_gradient * normalized_input, axis=(0, 1, 2)),
        ),
        ("space", "batch"),
    )
    first_layer_gradient = (
        ocean_mask
        * batchnorm_gain
        * inverse_deviation
        * (
            preactivation_gradient
            - (offset_gradient + normalized_input * gain_gradient) / element_count
        )
    ).astype(jnp.bfloat16)
    grad_in = reduce_weights(tap_grads(padded_in, first_layer_gradient, lon, lat))
    return (output, grad_in, grad_out, gain_gradient, offset_gradient)


def solution(mesh):
    in_specs = (
        P(("groups", "batch"), "space", None, None),
        P("space", None),
        P(),
        P(),
        P(),
        P(),
        P(("groups", "batch"), "space", None, None),
    )
    out_specs = (
        P(("groups", "batch"), "space", None, None),
        P("groups", None, "batch"),
        P("groups", None, "batch"),
        P("groups"),
        P("groups"),
    )
    return jax.shard_map(body, mesh=mesh, in_specs=in_specs, out_specs=out_specs, check_vma=False)
```

profile of v0, /device:TPU:0, one launch (start us, length us, event | category | flops | bytes accessed | tf_op | source)
XLA Modules:
  0.0 216.1 jit_solution(872169914859820042)
XLA Ops:
  7.2 0.7 fusion.202
  7.9 1.0 broadcast_multiply_fusion
  9.0 3.1 %collective-permute-start = (bf16[1,8,128]{2,1,0:T(8,128)(2,1)S(1)}, bf16[1,8,128]{2,1,0:T(8,128)(2,1)S(1)}, u32[]{:S(2)}, u32[]{:S(2)}) collective-permute-start(bf16[1,8,128]{2,1,0:T(8,128)(2,1)S(1)} %bitcast.514), channel_id=1, source_target_pairs={{0,4},{4,0},{8,12},{12,8},{1,5},{5,1},{9,13},{13,9},{2,6},{6,2},{1... | collective-permute-start | bytes 6152 | tf_op jit(solution)/shard_map/ppermute | solution.py:10
  12.1 1.6 collective-permute-done
  13.7 3.0 %collective-permute-start.1 = (bf16[1,8,128]{2,1,0:T(8,128)(2,1)S(1)}, bf16[1,8,128]{2,1,0:T(8,128)(2,1)S(1)}, u32[]{:S(2)}, u32[]{:S(2)}) collective-permute-start(bf16[1,8,128]{2,1,0:T(8,128)(2,1)S(1)} %collective-permute-done), channel_id=1, source_target_pairs={{0,8},{4,12},{8,0},{12,4},{1,9},{5,13},{9,1},{13,5},{2,10},{6,14},... | collective-permute-start | bytes 6152 | tf_op jit(solution)/shard_map/ppermute | solution.py:10
  17.4 0.9 collective-permute-done.1
  18.4 4.0 %collective-permute-start.3 = (bf16[1,1,66,128]{3,2,1,0:T(8,128)(2,1)S(1)}, bf16[1,1,66,128]{3,2,1,0:T(8,128)(2,1)S(1)}, u32[]{:S(2)}, u32[]{:S(2)}) collective-permute-start(bf16[1,1,66,128]{3,2,1,0:T(8,128)(2,1)S(1)} %get-tuple-element.94), channel_id=1, source_target_pairs={{4,0},{8,4},{12,8},{0,12},{5,1},{9,5},{13,9},{1,13},{6,2},{10,6},{... | collective-permute-start | bytes 50696 | tf_op jit(solution)/shard_map/ppermute | solution.py:21
  22.4 1.4 collective-permute-done.3
  23.8 4.1 %collective-permute-done.2 = bf16[1,1,66,128]{3,2,1,0:T(8,128)(2,1)S(1)} collective-permute-done((bf16[1,1,66,128]{3,2,1,0:T(8,128)(2,1)S(1)}, bf16[1,1,66,128]{3,2,1,0:T(8,128)(2,1)S(1)}, u32[]{:S(2)}, u32[]{:S(2)}) %collective-permute-start.2) | collective-permute-done | bytes 16928 | tf_op jit(solution)/shard_map/ppermute | solution.py:20
  28.2 0.8 copy-done.1
  30.6 30.1 %all-reduce.3 = (f32[]{:T(128)}, f32[128]{0:T(128)S(1)}, f32[128]{0:T(128)S(1)}) all-reduce(f32[]{:T(128)} %convert_reduce_fusion, f32[128]{0:T(128)S(1)} %get-tuple-element.55, f32[128]{0:T(128)S(1)} %get-tuple-element.54), channel_id=1, replica_groups=mesh['groups'=2,'space'=4,'batch'=4] {'space','batch'}, use_global_device_ids=true, to_apply=%region_3.4 | all-reduce | flops 257 | bytes 2056 | tf_op jit(solution)/shard_map/psum | solution.py:119
  61.7 3.6 %collective-permute-done.8 = bf16[1,8,128]{2,1,0:T(8,128)(2,1)S(1)} collective-permute-done((bf16[1,8,128]{2,1,0:T(8,128)(2,1)S(1)}, bf16[1,8,128]{2,1,0:T(8,128)(2,1)S(1)}, u32[]{:S(2)}, u32[]{:S(2)}) %collective-permute-start.8) | collective-permute-done | bytes 2080 | tf_op jit(solution)/shard_map/ppermute | solution.py:10
  65.3 4.5 %collective-permute-done.9 = bf16[1,8,128]{2,1,0:T(8,128)(2,1)S(1)} collective-permute-done((bf16[1,8,128]{2,1,0:T(8,128)(2,1)S(1)}, bf16[1,8,128]{2,1,0:T(8,128)(2,1)S(1)}, u32[]{:S(2)}, u32[]{:S(2)}) %collective-permute-start.9) | collective-permute-done | bytes 2080 | tf_op jit(solution)/shard_map/ppermute | solution.py:10
  69.9 2.0 collective-permute-start.10
  71.9 0.7 add_rsqrt_fusion
  72.6 1.1 collective-permute-done.11
  73.6 1.9 collective-permute-done.10
  75.9 0.7 copy-done
  78.9 0.6 copy-done.5
  80.1 3.4 %collective-permute-done.4 = bf16[1,8,128]{2,1,0:T(8,128)(2,1)S(1)} collective-permute-done((bf16[1,8,128]{2,1,0:T(8,128)(2,1)S(1)}, bf16[1,8,128]{2,1,0:T(8,128)(2,1)S(1)}, u32[]{:S(2)}, u32[]{:S(2)}) %collective-permute-start.4) | collective-permute-done | bytes 2080 | tf_op jit(solution)/shard_map/ppermute | solution.py:10
  83.6 29.5 %all-reduce.2 = (f32[128]{0:T(128)S(1)}, f32[128]{0:T(128)S(1)}) all-reduce(f32[128]{0:T(128)S(1)} %get-tuple-element.57, f32[128]{0:T(128)S(1)} %get-tuple-element.56), channel_id=1, replica_groups=mesh['groups'=2,'space'=4,'batch'=4] {'space','batch'}, use_global_device_ids=true, to_apply=%region_9.10 | all-reduce | flops 256 | bytes 2048 | tf_op jit(solution)/shard_map/psum | solution.py:141
  113.3 2.0 collective-permute-start.6
  115.4 1.7 collective-permute-done.7
  117.1 1.9 collective-permute-done.6
  121.0 1.5 multiply_convert_fusion
  124.7 1.2 copy.85
  128.0 1.2 copy.86
  129.3 15.8 %reduce-scatter.3.cloned.1.call-done = bf16[9,128,32]{1,0,2:T(8,128)(2,1)} async-done(((bf16[9,128,128]{1,0,2:T(8,128)(2,1)}), bf16[9,128,32]{1,0,2:T(8,128)(2,1)}) %reduce-scatter.3.cloned.1.call-update) | async-done | bytes 73744 | tf_op jit(solution)/shard_map/reduce_scatter | solution.py:95
  145.0 24.2 %reduce-scatter.5.cloned.1.call-done = bf16[9,128,32]{1,0,2:T(8,128)(2,1)} async-done(((bf16[9,128,128]{1,0,2:T(8,128)(2,1)}), bf16[9,128,32]{1,0,2:T(8,128)(2,1)}) %reduce-scatter.5.cloned.1.call-update) | async-done | bytes 73744 | tf_op jit(solution)/shard_map/reduce_scatter | solution.py:95
  169.2 38.1 %all-reduce.7.cloned.1.call-done = (bf16[9,128,32]{1,0,2:T(8,128)(2,1)}, bf16[9,128,32]{1,0,2:T(8,128)(2,1)}) async-done(((bf16[9,128,32]{1,0,2:T(8,128)(2,1)}, bf16[9,128,32]{1,0,2:T(8,128)(2,1)}), (bf16[9,128,32]{1,0,2:T(8,128)(2,1)}, bf16[9,128,32]{1,0,2:T(8,128)(2,1)})) %all-reduce.7.cloned.1.call-update) | async-done | bytes 147472 | tf_op jit(solution)/shard_map/psum | solution.py:94
  207.3 1.6 copy.87
  208.9 0.7 copy.88
  (116 shorter events, 12.8 us)
Async XLA Ops:
  7.2 137.9 %reduce-scatter.3.cloned.1.call-start = ((), (), s32[]{:S(2)}) async-start(), calls=%async_computation.2 | async-start | bytes 655360 | tf_op jit(solution)/shard_map/reduce_scatter | solution.py:95
  9.0 7.7 %copy-start.4 = (s32[8,64]{1,0:T(8,128)S(1)}, s32[8,64]{1,0:T(8,128)}, u32[]{:S(2)}) copy-start(s32[8,64]{1,0:T(8,128)} %param.12) | copy-start | bytes 6148
  9.0 4.7 %collective-permute-start = (bf16[1,8,128]{2,1,0:T(8,128)(2,1)S(1)}, bf16[1,8,128]{2,1,0:T(8,128)(2,1)S(1)}, u32[]{:S(2)}, u32[]{:S(2)}) collective-permute-start(bf16[1,8,128]{2,1,0:T(8,128)(2,1)S(1)} %bitcast.514), channel_id=1, source_target_pairs={{0,4},{4,0},{8,12},{12,8},{1,5},{5,1},{9,13},{13,9},{2,6},{6,2},{1... | collective-permute-start | bytes 6152 | tf_op jit(solution)/shard_map/ppermute | solution.py:10
  13.7 4.6 %collective-permute-start.1 = (bf16[1,8,128]{2,1,0:T(8,128)(2,1)S(1)}, bf16[1,8,128]{2,1,0:T(8,128)(2,1)S(1)}, u32[]{:S(2)}, u32[]{:S(2)}) collective-permute-start(bf16[1,8,128]{2,1,0:T(8,128)(2,1)S(1)} %collective-permute-done), channel_id=1, source_target_pairs={{0,8},{4,12},{8,0},{12,4},{1,9},{5,13},{9,1},{13,5},{2,10},{6,14},... | collective-permute-start | bytes 6152 | tf_op jit(solution)/shard_map/ppermute | solution.py:10
  18.4 5.5 %collective-permute-start.3 = (bf16[1,1,66,128]{3,2,1,0:T(8,128)(2,1)S(1)}, bf16[1,1,66,128]{3,2,1,0:T(8,128)(2,1)S(1)}, u32[]{:S(2)}, u32[]{:S(2)}) collective-permute-start(bf16[1,1,66,128]{3,2,1,0:T(8,128)(2,1)S(1)} %get-tuple-element.94), channel_id=1, source_target_pairs={{4,0},{8,4},{12,8},{0,12},{5,1},{9,5},{13,9},{1,13},{6,2},{10,6},{... | collective-permute-start | bytes 50696 | tf_op jit(solution)/shard_map/ppermute | solution.py:21
  22.4 5.6 %collective-permute-start.2 = (bf16[1,1,66,128]{3,2,1,0:T(8,128)(2,1)S(1)}, bf16[1,1,66,128]{3,2,1,0:T(8,128)(2,1)S(1)}, u32[]{:S(2)}, u32[]{:S(2)}) collective-permute-start(bf16[1,1,66,128]{3,2,1,0:T(8,128)(2,1)S(1)} %get-tuple-element.95), channel_id=1, source_target_pairs={{0,4},{4,8},{8,12},{12,0},{1,5},{5,9},{9,13},{13,1},{2,6},{6,10},{... | collective-permute-start | bytes 50696 | tf_op jit(solution)/shard_map/ppermute | solution.py:20
  28.0 1.0 copy-start.1
  30.4 31.1 %copy-start.2 = (bf16[1,8,64,128]{3,2,1,0:T(8,128)(2,1)S(1)}, bf16[1,8,64,128]{3,2,1,0:T(8,128)(2,1)}, u32[]{:S(2)}) copy-start(bf16[1,8,64,128]{3,2,1,0:T(8,128)(2,1)} %param.17) | copy-start | bytes 393220
  61.6 3.7 %collective-permute-start.8 = (bf16[1,8,128]{2,1,0:T(8,128)(2,1)S(1)}, bf16[1,8,128]{2,1,0:T(8,128)(2,1)S(1)}, u32[]{:S(2)}, u32[]{:S(2)}) collective-permute-start(bf16[1,8,128]{2,1,0:T(8,128)(2,1)S(1)} %bitcast.515), channel_id=1, source_target_pairs={{0,4},{4,0},{8,12},{12,8},{1,5},{5,1},{9,13},{13,9},{2,6},{6,2},{1... | collective-permute-start | bytes 6152 | tf_op jit(solution)/shard_map/ppermute | solution.py:10
  65.3 4.5 %collective-permute-start.9 = (bf16[1,8,128]{2,1,0:T(8,128)(2,1)S(1)}, bf16[1,8,128]{2,1,0:T(8,128)(2,1)S(1)}, u32[]{:S(2)}, u32[]{:S(2)}) collective-permute-start(bf16[1,8,128]{2,1,0:T(8,128)(2,1)S(1)} %collective-permute-done.8), channel_id=1, source_target_pairs={{0,8},{4,12},{8,0},{12,4},{1,9},{5,13},{9,1},{13,5},{2,10},{6,14},... | collective-permute-start | bytes 6152 | tf_op jit(solution)/shard_map/ppermute | solution.py:10
  69.8 3.8 %collective-permute-start.11 = (bf16[1,1,66,128]{3,2,1,0:T(8,128)(2,1)S(1)}, bf16[1,1,66,128]{3,2,1,0:T(8,128)(2,1)S(1)}, u32[]{:S(2)}, u32[]{:S(2)}) collective-permute-start(bf16[1,1,66,128]{3,2,1,0:T(8,128)(2,1)S(1)} %get-tuple-element.91), channel_id=1, source_target_pairs={{4,0},{8,4},{12,8},{0,12},{5,1},{9,5},{13,9},{1,13},{6,2},{10,6},{... | collective-permute-start | bytes 50696 | tf_op jit(solution)/shard_map/ppermute | solution.py:21
  69.9 5.6 %collective-permute-start.10 = (bf16[1,1,66,128]{3,2,1,0:T(8,128)(2,1)S(1)}, bf16[1,1,66,128]{3,2,1,0:T(8,128)(2,1)S(1)}, u32[]{:S(2)}, u32[]{:S(2)}) collective-permute-start(bf16[1,1,66,128]{3,2,1,0:T(8,128)(2,1)S(1)} %get-tuple-element.90), channel_id=1, source_target_pairs={{0,4},{4,8},{8,12},{12,0},{1,5},{5,9},{9,13},{13,1},{2,6},{6,10},{... | collective-permute-start | bytes 50696 | tf_op jit(solution)/shard_map/ppermute | solution.py:20
  75.7 1.0 copy-start
  78.9 0.7 copy-start.5
  78.9 0.7 copy-start.6
  79.8 3.7 %collective-permute-start.4 = (bf16[1,8,128]{2,1,0:T(8,128)(2,1)S(1)}, bf16[1,8,128]{2,1,0:T(8,128)(2,1)S(1)}, u32[]{:S(2)}, u32[]{:S(2)}) collective-permute-start(bf16[1,8,128]{2,1,0:T(8,128)(2,1)S(1)} %bitcast.516), channel_id=1, source_target_pairs={{0,4},{4,0},{8,12},{12,8},{1,5},{5,1},{9,13},{13,9},{2,6},{6,2},{1... | collective-permute-start | bytes 6152 | tf_op jit(solution)/shard_map/ppermute | solution.py:10
  83.5 29.6 %collective-permute-start.5 = (bf16[1,8,128]{2,1,0:T(8,128)(2,1)S(1)}, bf16[1,8,128]{2,1,0:T(8,128)(2,1)S(1)}, u32[]{:S(2)}, u32[]{:S(2)}) collective-permute-start(bf16[1,8,128]{2,1,0:T(8,128)(2,1)S(1)} %collective-permute-done.4), channel_id=1, source_target_pairs={{0,8},{4,12},{8,0},{12,4},{1,9},{5,13},{9,1},{13,5},{2,10},{6,14},... | collective-permute-start | bytes 6152 | tf_op jit(solution)/shard_map/ppermute | solution.py:10
  113.1 7.9 %copy-start.7 = (f32[128]{0:T(128)}, f32[128]{0:T(128)S(1)}, u32[]{:S(2)}) copy-start(f32[128]{0:T(128)S(1)} %get-tuple-element.58) | copy-start | bytes 1540
  113.1 7.9 %copy-start.8 = (f32[128]{0:T(128)}, f32[128]{0:T(128)S(1)}, u32[]{:S(2)}) copy-start(f32[128]{0:T(128)S(1)} %get-tuple-element.59) | copy-start | bytes 1540
  113.2 3.8 %collective-permute-start.7 = (bf16[1,1,66,128]{3,2,1,0:T(8,128)(2,1)S(1)}, bf16[1,1,66,128]{3,2,1,0:T(8,128)(2,1)S(1)}, u32[]{:S(2)}, u32[]{:S(2)}) collective-permute-start(bf16[1,1,66,128]{3,2,1,0:T(8,128)(2,1)S(1)} %get-tuple-element.92), channel_id=1, source_target_pairs={{4,0},{8,4},{12,8},{0,12},{5,1},{9,5},{13,9},{1,13},{6,2},{10,6},{... | collective-permute-start | bytes 50696 | tf_op jit(solution)/shard_map/ppermute | solution.py:21
  113.3 5.6 %collective-permute-start.6 = (bf16[1,1,66,128]{3,2,1,0:T(8,128)(2,1)S(1)}, bf16[1,1,66,128]{3,2,1,0:T(8,128)(2,1)S(1)}, u32[]{:S(2)}, u32[]{:S(2)}) collective-permute-start(bf16[1,1,66,128]{3,2,1,0:T(8,128)(2,1)S(1)} %get-tuple-element.93), channel_id=1, source_target_pairs={{0,4},{4,8},{8,12},{12,0},{1,5},{5,9},{9,13},{13,1},{2,6},{6,10},{... | collective-permute-start | bytes 50696 | tf_op jit(solution)/shard_map/ppermute | solution.py:20
  125.9 43.3 %reduce-scatter.5.cloned.1.call-start = ((), (), s32[]{:S(2)}) async-start(), calls=%async_computation.3 | async-start | bytes 655360 | tf_op jit(solution)/shard_map/reduce_scatter | solution.py:95
  129.2 78.1 %all-reduce.7.cloned.1.call-start = ((), (), s32[]{:S(2)}) async-start(), calls=%async_computation.4 | async-start | bytes 524288 | tf_op jit(solution)/shard_map/psum | solution.py:94
  207.3 1.6 copy-start.3
Sparse Core Ops, SparseCore 0:
  126.0 18.9 reduce-scatter.2
  147.5 21.6 reduce-scatter.4
  171.6 35.6 all-reduce.6
where the time goes:
time: 216 us
  waiting for transfers between devices  104 us (48%)
  blocking collectives  59.6 us (28%)
  between operations  15 us (7%)
  starting transfers between devices  14.7 us (7%)
  matrix products  9.6 us (4%)
  local copies, waits for them, and re-layouts  7.76 us (4%)
  other arithmetic  5.5 us (3%)
    reduce_scatter x2, waiting for transfers between devices, reduce_weights(): lax.psum_scatter(summed, 'batch', scatter_dimension=2, tiled=True)  39.9 us
    psum x1, waiting for transfers between devices, reduce_weights(): summed = lax.psum(partial_grad.astype(jnp.bfloat16), 'space')  38.1 us
    psum x1, blocking collectives, body(): lax.psum((jnp.sum(first_features * ocean_mask, axis=(0, 1, 2)), jnp.sum(f...  30.1 us
    psum x1, blocking collectives, body(): lax.psum((jnp.sum(preactivation_gradient, axis=(0, 1, 2)), jnp.sum(preact...  29.5 us
    ppermute x6, waiting for transfers between devices, partner(): return lax.ppermute(value, axis, pairs)  13.9 us
    ppermute x3, waiting for transfers between devices, extended_2(): before = lax.ppermute(last, axis, up)  7.82 us
    ppermute x6, starting transfers between devices, partner(): return lax.ppermute(value, axis, pairs)  6.46 us
    unnamed x24, local copies, waits for them, and re-layouts  4.49 us
  transfers between devices with their start and end apart: 15, of which 14 were waited for; matrix products, arithmetic and copies ran while one was open for 2% of the time, Pallas kernels for 0%

commit v1 on v0

--- a/solution.py
+++ b/solution.py
@@ -139,11 +139,14 @@
     dact = adjoint_conv(surround(dout), conv_out, lon, lat)
     preactivation_gradient = dact * ocean_mask * gelu_slope(preactivation)
     offset_gradient, gain_gradient = lax.psum(
-        (
-            jnp.sum(preactivation_gradient, axis=(0, 1, 2)),
-            jnp.sum(preactivation_gradient * normalized_input, axis=(0, 1, 2)),
+        lax.psum(
+            (
+                jnp.sum(preactivation_gradient, axis=(0, 1, 2)),
+                jnp.sum(preactivation_gradient * normalized_input, axis=(0, 1, 2)),
+            ),
+            "batch",
         ),
-        ("space", "batch"),
+        "space",
     )
     first_layer_gradient = (
         ocean_mask

time: 216 us -> 204 us (0.944)
  blocking collectives: 59.6 us -> 46.8 us
    psum x1, blocking collectives: 29.5 us -> 5.76 us  [body(): lax.psum((jnp.sum(preactivation_gradient, axis=(0, 1, 2)), jnp.sum(preact...]
    psum x0 -> x1, blocking collectives: none -> 10.9 us  [body(): lax.psum(lax.psum((jnp.sum(preactivation_gradient, axis=(0, 1, 2)), jnp.s...]
where the time goes in v1:
time: 204 us; the launch traced here: 203 us
  waiting for transfers between devices  104 us (51%)
  blocking collectives  46.8 us (23%)
  between operations  15 us (7%)
  starting transfers between devices  14.7 us (7%)
  matrix products  9.59 us (5%)
  local copies, waits for them, and re-layouts  7.79 us (4%)
  other arithmetic  5.5 us (3%)
    reduce_scatter x2, waiting for transfers between devices, reduce_weights(): lax.psum_scatter(summed, 'batch', scatter_dimension=2, tiled=True)  39.9 us
    psum x1, waiting for transfers between devices, reduce_weights(): summed = lax.psum(partial_grad.astype(jnp.bfloat16), 'space')  38 us
    psum x1, blocking collectives, body(): lax.psum((jnp.sum(first_features * ocean_mask, axis=(0, 1, 2)), jnp.sum(f...  30.1 us
    ppermute x6, waiting for transfers between devices, partner(): return lax.ppermute(value, axis, pairs)  13.9 us
    psum x1, blocking collectives, body(): lax.psum(lax.psum((jnp.sum(preactivation_gradient, axis=(0, 1, 2)), jnp.s...  10.9 us
    ppermute x3, waiting for transfers between devices, extended_2(): before = lax.ppermute(last, axis, up)  7.82 us
    ppermute x6, starting transfers between devices, partner(): return lax.ppermute(value, axis, pairs)  6.46 us
    psum x1, blocking collectives, body(): lax.psum((jnp.sum(preactivation_gradient, axis=(0, 1, 2)), jnp.sum(preact...  5.76 us
  transfers between devices with their start and end apart: 15, of which 14 were waited for; matrix products, arithmetic and copies ran while one was open for 2% of the time, Pallas kernels for 0%

profile of v1, /device:TPU:0, one launch (start us, length us, event | category | flops | bytes accessed | tf_op | source)
XLA Modules:
  0.0 203.3 jit_solution(1629398224299975106)
XLA Ops:
  7.2 0.7 fusion.202
  7.9 1.0 broadcast_multiply_fusion
  9.0 3.1 %collective-permute-start = (bf16[1,8,128]{2,1,0:T(8,128)(2,1)S(1)}, bf16[1,8,128]{2,1,0:T(8,128)(2,1)S(1)}, u32[]{:S(2)}, u32[]{:S(2)}) collective-permute-start(bf16[1,8,128]{2,1,0:T(8,128)(2,1)S(1)} %bitcast.514), channel_id=1, source_target_pairs={{0,4},{4,0},{8,12},{12,8},{1,5},{5,1},{9,13},{13,9},{2,6},{6,2},{1... | collective-permute-start | bytes 6152 | tf_op jit(solution)/shard_map/ppermute | solution.py:10
  12.1 1.6 collective-permute-done
  13.7 3.0 %collective-permute-start.1 = (bf16[1,8,128]{2,1,0:T(8,128)(2,1)S(1)}, bf16[1,8,128]{2,1,0:T(8,128)(2,1)S(1)}, u32[]{:S(2)}, u32[]{:S(2)}) collective-permute-start(bf16[1,8,128]{2,1,0:T(8,128)(2,1)S(1)} %collective-permute-done), channel_id=1, source_target_pairs={{0,8},{4,12},{8,0},{12,4},{1,9},{5,13},{9,1},{13,5},{2,10},{6,14},... | collective-permute-start | bytes 6152 | tf_op jit(solution)/shard_map/ppermute | solution.py:10
  17.4 0.9 collective-permute-done.1
  18.4 4.0 %collective-permute-start.3 = (bf16[1,1,66,128]{3,2,1,0:T(8,128)(2,1)S(1)}, bf16[1,1,66,128]{3,2,1,0:T(8,128)(2,1)S(1)}, u32[]{:S(2)}, u32[]{:S(2)}) collective-permute-start(bf16[1,1,66,128]{3,2,1,0:T(8,128)(2,1)S(1)} %get-tuple-element.96), channel_id=1, source_target_pairs={{4,0},{8,4},{12,8},{0,12},{5,1},{9,5},{13,9},{1,13},{6,2},{10,6},{... | collective-permute-start | bytes 50696 | tf_op jit(solution)/shard_map/ppermute | solution.py:21
  22.4 1.4 collective-permute-done.3
  23.8 4.1 %collective-permute-done.2 = bf16[1,1,66,128]{3,2,1,0:T(8,128)(2,1)S(1)} collective-permute-done((bf16[1,1,66,128]{3,2,1,0:T(8,128)(2,1)S(1)}, bf16[1,1,66,128]{3,2,1,0:T(8,128)(2,1)S(1)}, u32[]{:S(2)}, u32[]{:S(2)}) %collective-permute-start.2) | collective-permute-done | bytes 16928 | tf_op jit(solution)/shard_map/ppermute | solution.py:20
  28.2 0.8 copy-done.1
  30.6 30.1 %all-reduce.2 = (f32[]{:T(128)}, f32[128]{0:T(128)S(1)}, f32[128]{0:T(128)S(1)}) all-reduce(f32[]{:T(128)} %convert_reduce_fusion, f32[128]{0:T(128)S(1)} %get-tuple-element.55, f32[128]{0:T(128)S(1)} %get-tuple-element.54), channel_id=1, replica_groups=mesh['groups'=2,'space'=4,'batch'=4] {'space','batch'}, use_global_device_ids=true, to_apply=%region_3.4 | all-reduce | flops 257 | bytes 2056 | tf_op jit(solution)/shard_map/psum | solution.py:119
  61.7 3.6 %collective-permute-done.8 = bf16[1,8,128]{2,1,0:T(8,128)(2,1)S(1)} collective-permute-done((bf16[1,8,128]{2,1,0:T(8,128)(2,1)S(1)}, bf16[1,8,128]{2,1,0:T(8,128)(2,1)S(1)}, u32[]{:S(2)}, u32[]{:S(2)}) %collective-permute-start.8) | collective-permute-done | bytes 2080 | tf_op jit(solution)/shard_map/ppermute | solution.py:10
  65.3 4.5 %collective-permute-done.9 = bf16[1,8,128]{2,1,0:T(8,128)(2,1)S(1)} collective-permute-done((bf16[1,8,128]{2,1,0:T(8,128)(2,1)S(1)}, bf16[1,8,128]{2,1,0:T(8,128)(2,1)S(1)}, u32[]{:S(2)}, u32[]{:S(2)}) %collective-permute-start.9) | collective-permute-done | bytes 2080 | tf_op jit(solution)/shard_map/ppermute | solution.py:10
  69.9 2.0 collective-permute-start.10
  71.9 0.7 add_rsqrt_fusion
  72.6 1.1 collective-permute-done.11
  73.6 1.9 collective-permute-done.10
  75.9 0.7 copy-done
  80.1 3.4 %collective-permute-done.4 = bf16[1,8,128]{2,1,0:T(8,128)(2,1)S(1)} collective-permute-done((bf16[1,8,128]{2,1,0:T(8,128)(2,1)S(1)}, bf16[1,8,128]{2,1,0:T(8,128)(2,1)S(1)}, u32[]{:S(2)}, u32[]{:S(2)}) %collective-permute-start.4) | collective-permute-done | bytes 2080 | tf_op jit(solution)/shard_map/ppermute | solution.py:10
  83.6 5.8 %all-reduce.3 = (f32[128]{0:T(128)S(1)}, f32[128]{0:T(128)S(1)}) all-reduce(f32[128]{0:T(128)S(1)} %get-tuple-element.57, f32[128]{0:T(128)S(1)} %get-tuple-element.56), channel_id=1, replica_groups=mesh['groups'=2,'space'=4,'batch'=4] {'batch'}, use_global_device_ids=true, to_apply=%region_10.11 | all-reduce | flops 256 | bytes 2048 | tf_op jit(solution)/shard_map/psum | solution.py:142
  89.4 10.9 %all-reduce.4 = (f32[128]{0:T(128)S(1)}, f32[128]{0:T(128)S(1)}) all-reduce(f32[128]{0:T(128)S(1)} %get-tuple-element.61, f32[128]{0:T(128)S(1)} %get-tuple-element.62), channel_id=1, replica_groups=mesh['groups'=2,'space'=4,'batch'=4] {'space'}, use_global_device_ids=true, to_apply=%region_11.12 | all-reduce | flops 256 | bytes 2048 | tf_op jit(solution)/shard_map/psum | solution.py:141
  100.5 2.0 collective-permute-start.6
  102.5 1.7 collective-permute-done.7
  104.2 1.9 collective-permute-done.6
  108.1 1.5 multiply_convert_fusion
  111.8 1.2 copy.85
  115.1 1.2 copy.86
  116.4 15.8 %reduce-scatter.3.cloned.1.call-done = bf16[9,128,32]{1,0,2:T(8,128)(2,1)} async-done(((bf16[9,128,128]{1,0,2:T(8,128)(2,1)}), bf16[9,128,32]{1,0,2:T(8,128)(2,1)}) %reduce-scatter.3.cloned.1.call-update) | async-done | bytes 73744 | tf_op jit(solution)/shard_map/reduce_scatter | solution.py:95
  132.2 24.2 %reduce-scatter.5.cloned.1.call-done = bf16[9,128,32]{1,0,2:T(8,128)(2,1)} async-done(((bf16[9,128,128]{1,0,2:T(8,128)(2,1)}), bf16[9,128,32]{1,0,2:T(8,128)(2,1)}) %reduce-scatter.5.cloned.1.call-update) | async-done | bytes 73744 | tf_op jit(solution)/shard_map/reduce_scatter | solution.py:95
  156.4 38.0 %all-reduce.8.cloned.1.call-done = (bf16[9,128,32]{1,0,2:T(8,128)(2,1)}, bf16[9,128,32]{1,0,2:T(8,128)(2,1)}) async-done(((bf16[9,128,32]{1,0,2:T(8,128)(2,1)}, bf16[9,128,32]{1,0,2:T(8,128)(2,1)}), (bf16[9,128,32]{1,0,2:T(8,128)(2,1)}, bf16[9,128,32]{1,0,2:T(8,128)(2,1)})) %all-reduce.8.cloned.1.call-update) | async-done | bytes 147472 | tf_op jit(solution)/shard_map/psum | solution.py:94
  194.4 1.6 copy.87
  196.0 0.7 copy.88
  (117 shorter events, 13.5 us)
Async XLA Ops:
  7.2 125.0 %reduce-scatter.3.cloned.1.call-start = ((), (), s32[]{:S(2)}) async-start(), calls=%async_computation.2 | async-start | bytes 655360 | tf_op jit(solution)/shard_map/reduce_scatter | solution.py:95
  9.0 7.7 %copy-start.4 = (s32[8,64]{1,0:T(8,128)S(1)}, s32[8,64]{1,0:T(8,128)}, u32[]{:S(2)}) copy-start(s32[8,64]{1,0:T(8,128)} %param.12) | copy-start | bytes 6148
  9.0 4.7 %collective-permute-start = (bf16[1,8,128]{2,1,0:T(8,128)(2,1)S(1)}, bf16[1,8,128]{2,1,0:T(8,128)(2,1)S(1)}, u32[]{:S(2)}, u32[]{:S(2)}) collective-permute-start(bf16[1,8,128]{2,1,0:T(8,128)(2,1)S(1)} %bitcast.514), channel_id=1, source_target_pairs={{0,4},{4,0},{8,12},{12,8},{1,5},{5,1},{9,13},{13,9},{2,6},{6,2},{1... | collective-permute-start | bytes 6152 | tf_op jit(solution)/shard_map/ppermute | solution.py:10
  13.7 4.6 %collective-permute-start.1 = (bf16[1,8,128]{2,1,0:T(8,128)(2,1)S(1)}, bf16[1,8,128]{2,1,0:T(8,128)(2,1)S(1)}, u32[]{:S(2)}, u32[]{:S(2)}) collective-permute-start(bf16[1,8,128]{2,1,0:T(8,128)(2,1)S(1)} %collective-permute-done), channel_id=1, source_target_pairs={{0,8},{4,12},{8,0},{12,4},{1,9},{5,13},{9,1},{13,5},{2,10},{6,14},... | collective-permute-start | bytes 6152 | tf_op jit(solution)/shard_map/ppermute | solution.py:10
  18.4 5.5 %collective-permute-start.3 = (bf16[1,1,66,128]{3,2,1,0:T(8,128)(2,1)S(1)}, bf16[1,1,66,128]{3,2,1,0:T(8,128)(2,1)S(1)}, u32[]{:S(2)}, u32[]{:S(2)}) collective-permute-start(bf16[1,1,66,128]{3,2,1,0:T(8,128)(2,1)S(1)} %get-tuple-element.96), channel_id=1, source_target_pairs={{4,0},{8,4},{12,8},{0,12},{5,1},{9,5},{13,9},{1,13},{6,2},{10,6},{... | collective-permute-start | bytes 50696 | tf_op jit(solution)/shard_map/ppermute | solution.py:21
  22.4 5.6 %collective-permute-start.2 = (bf16[1,1,66,128]{3,2,1,0:T(8,128)(2,1)S(1)}, bf16[1,1,66,128]{3,2,1,0:T(8,128)(2,1)S(1)}, u32[]{:S(2)}, u32[]{:S(2)}) collective-permute-start(bf16[1,1,66,128]{3,2,1,0:T(8,128)(2,1)S(1)} %get-tuple-element.97), channel_id=1, source_target_pairs={{0,4},{4,8},{8,12},{12,0},{1,5},{5,9},{9,13},{13,1},{2,6},{6,10},{... | collective-permute-start | bytes 50696 | tf_op jit(solution)/shard_map/ppermute | solution.py:20
  28.0 1.0 copy-start.1
  30.4 31.1 %copy-start.2 = (bf16[1,8,64,128]{3,2,1,0:T(8,128)(2,1)S(1)}, bf16[1,8,64,128]{3,2,1,0:T(8,128)(2,1)}, u32[]{:S(2)}) copy-start(bf16[1,8,64,128]{3,2,1,0:T(8,128)(2,1)} %param.17) | copy-start | bytes 393220
  61.6 3.7 %collective-permute-start.8 = (bf16[1,8,128]{2,1,0:T(8,128)(2,1)S(1)}, bf16[1,8,128]{2,1,0:T(8,128)(2,1)S(1)}, u32[]{:S(2)}, u32[]{:S(2)}) collective-permute-start(bf16[1,8,128]{2,1,0:T(8,128)(2,1)S(1)} %bitcast.515), channel_id=1, source_target_pairs={{0,4},{4,0},{8,12},{12,8},{1,5},{5,1},{9,13},{13,9},{2,6},{6,2},{1... | collective-permute-start | bytes 6152 | tf_op jit(solution)/shard_map/ppermute | solution.py:10
  65.3 4.5 %collective-permute-start.9 = (bf16[1,8,128]{2,1,0:T(8,128)(2,1)S(1)}, bf16[1,8,128]{2,1,0:T(8,128)(2,1)S(1)}, u32[]{:S(2)}, u32[]{:S(2)}) collective-permute-start(bf16[1,8,128]{2,1,0:T(8,128)(2,1)S(1)} %collective-permute-done.8), channel_id=1, source_target_pairs={{0,8},{4,12},{8,0},{12,4},{1,9},{5,13},{9,1},{13,5},{2,10},{6,14},... | collective-permute-start | bytes 6152 | tf_op jit(solution)/shard_map/ppermute | solution.py:10
  69.8 3.8 %collective-permute-start.11 = (bf16[1,1,66,128]{3,2,1,0:T(8,128)(2,1)S(1)}, bf16[1,1,66,128]{3,2,1,0:T(8,128)(2,1)S(1)}, u32[]{:S(2)}, u32[]{:S(2)}) collective-permute-start(bf16[1,1,66,128]{3,2,1,0:T(8,128)(2,1)S(1)} %get-tuple-element.93), channel_id=1, source_target_pairs={{4,0},{8,4},{12,8},{0,12},{5,1},{9,5},{13,9},{1,13},{6,2},{10,6},{... | collective-permute-start | bytes 50696 | tf_op jit(solution)/shard_map/ppermute | solution.py:21
  69.9 5.6 %collective-permute-start.10 = (bf16[1,1,66,128]{3,2,1,0:T(8,128)(2,1)S(1)}, bf16[1,1,66,128]{3,2,1,0:T(8,128)(2,1)S(1)}, u32[]{:S(2)}, u32[]{:S(2)}) collective-permute-start(bf16[1,1,66,128]{3,2,1,0:T(8,128)(2,1)S(1)} %get-tuple-element.92), channel_id=1, source_target_pairs={{0,4},{4,8},{8,12},{12,0},{1,5},{5,9},{9,13},{13,1},{2,6},{6,10},{... | collective-permute-start | bytes 50696 | tf_op jit(solution)/shard_map/ppermute | solution.py:20
  75.7 1.0 copy-start
  78.9 0.7 copy-start.5
  78.9 0.7 copy-start.6
  79.8 3.7 %collective-permute-start.4 = (bf16[1,8,128]{2,1,0:T(8,128)(2,1)S(1)}, bf16[1,8,128]{2,1,0:T(8,128)(2,1)S(1)}, u32[]{:S(2)}, u32[]{:S(2)}) collective-permute-start(bf16[1,8,128]{2,1,0:T(8,128)(2,1)S(1)} %bitcast.516), channel_id=1, source_target_pairs={{0,4},{4,0},{8,12},{12,8},{1,5},{5,1},{9,13},{13,9},{2,6},{6,2},{1... | collective-permute-start | bytes 6152 | tf_op jit(solution)/shard_map/ppermute | solution.py:10
  83.5 16.8 %collective-permute-start.5 = (bf16[1,8,128]{2,1,0:T(8,128)(2,1)S(1)}, bf16[1,8,128]{2,1,0:T(8,128)(2,1)S(1)}, u32[]{:S(2)}, u32[]{:S(2)}) collective-permute-start(bf16[1,8,128]{2,1,0:T(8,128)(2,1)S(1)} %collective-permute-done.4), channel_id=1, source_target_pairs={{0,8},{4,12},{8,0},{12,4},{1,9},{5,13},{9,1},{13,5},{2,10},{6,14},... | collective-permute-start | bytes 6152 | tf_op jit(solution)/shard_map/ppermute | solution.py:10
  100.3 7.9 %copy-start.7 = (f32[128]{0:T(128)}, f32[128]{0:T(128)S(1)}, u32[]{:S(2)}) copy-start(f32[128]{0:T(128)S(1)} %get-tuple-element.63) | copy-start | bytes 1540
  100.3 7.9 %copy-start.8 = (f32[128]{0:T(128)}, f32[128]{0:T(128)S(1)}, u32[]{:S(2)}) copy-start(f32[128]{0:T(128)S(1)} %get-tuple-element.64) | copy-start | bytes 1540
  100.4 3.8 %collective-permute-start.7 = (bf16[1,1,66,128]{3,2,1,0:T(8,128)(2,1)S(1)}, bf16[1,1,66,128]{3,2,1,0:T(8,128)(2,1)S(1)}, u32[]{:S(2)}, u32[]{:S(2)}) collective-permute-start(bf16[1,1,66,128]{3,2,1,0:T(8,128)(2,1)S(1)} %get-tuple-element.94), channel_id=1, source_target_pairs={{4,0},{8,4},{12,8},{0,12},{5,1},{9,5},{13,9},{1,13},{6,2},{10,6},{... | collective-permute-start | bytes 50696 | tf_op jit(solution)/shard_map/ppermute | solution.py:21
  100.5 5.6 %collective-permute-start.6 = (bf16[1,1,66,128]{3,2,1,0:T(8,128)(2,1)S(1)}, bf16[1,1,66,128]{3,2,1,0:T(8,128)(2,1)S(1)}, u32[]{:S(2)}, u32[]{:S(2)}) collective-permute-start(bf16[1,1,66,128]{3,2,1,0:T(8,128)(2,1)S(1)} %get-tuple-element.95), channel_id=1, source_target_pairs={{0,4},{4,8},{8,12},{12,0},{1,5},{5,9},{9,13},{13,1},{2,6},{6,10},{... | collective-permute-start | bytes 50696 | tf_op jit(solution)/shard_map/ppermute | solution.py:20
  113.1 43.3 %reduce-scatter.5.cloned.1.call-start = ((), (), s32[]{:S(2)}) async-start(), calls=%async_computation.3 | async-start | bytes 655360 | tf_op jit(solution)/shard_map/reduce_scatter | solution.py:95
  116.4 78.1 %all-reduce.8.cloned.1.call-start = ((), (), s32[]{:S(2)}) async-start(), calls=%async_computation.4 | async-start | bytes 524288 | tf_op jit(solution)/shard_map/psum | solution.py:94
  194.4 1.6 copy-start.3
Sparse Core Ops, SparseCore 0:
  113.2 18.9 reduce-scatter.2
  134.7 21.6 reduce-scatter.4
  158.7 35.6 all-reduce.7
